TPU v7x, 32 devices: a whole 2x2x4 slice. The times are simulated.
32 devices in a mesh: bunch: 4 (over y, x), mp: 8 (over z, core).
Axes of the slice: x: 2, y: 2, z: 4, core: 2. Of those that a mesh axis runs over, the one named last changes fastest.
Arguments:
- phase_space: float32 [4, 64, 32768], P(None, 'bunch', 'mp')
- phase_advance: float32 [2, 64], P(None, 'bunch'), may hold values from 0.3 to 2.8
- centroid_history: float32 [2, 64, 64], P(None, None, 'bunch'), may hold values from -6 to 6
- lr_wake: float32 [4160], replicated, may hold values from -0.09375 to 0.09375
- sr_dipole: float32 [256, 256], replicated, may hold values from -24 to 24
- sr_quad: float32 [256, 256], replicated, may hold values from -24 to 24
- slice_ids: int32 [2, 64, 32768], P(None, 'bunch', 'mp'), may hold values from 0 to 255
Outputs:
- tracked: float32 [4, 64, 32768], P(None, 'bunch', 'mp')
- centroids: float32 [2, 2, 64], P(None, None, 'bunch')
All inputs are finite; a program needn't handle non-finite values.
Results may differ from a plain program's by a relative error of at most 0.00019.
Values sent between devices are 32-bit elements; how exact they have to be, the bound alone decides.
No kernel may reach another device: no remote copies, remote signals or barrier semaphores. Data moves between devices by JAX's collectives and lax.ppermute only.
A program may use at most 64 MiB of HBM per device.

v0:
```python
import jax
import jax.numpy as jnp
from jax import lax
from jax.sharding import PartitionSpec as P

SLICES = 256
TURNS = 2
DETUNE = 0.02


def body(phase_space, phase_advance, centroid_history, lr_wake, sr_dipole, sr_quad, slice_ids):
    highest = lax.Precision.HIGHEST
    bunch_dev = phase_space.shape[1]
    depth = centroid_history.shape[1]
    macro_total = phase_space.shape[2] * lax.axis_size("mp")
    all_bunches = bunch_dev * lax.axis_size("bunch")
    length = (depth + 1) * all_bunches
    offset_bunch = lax.axis_index("bunch") * bunch_dev
    own_index = jnp.arange(bunch_dev, dtype=jnp.int32)
    levels = jnp.arange(SLICES, dtype=jnp.int32)
    padded = jnp.concatenate([jnp.zeros((all_bunches,), jnp.float32), lr_wake])
    windows = jax.vmap(lambda start_at: lax.dynamic_slice(padded, (start_at,), (length,)))(
        offset_bunch + own_index
    )
    history = centroid_history
    whole = lax.all_gather(centroid_history, "bunch", axis=2, tiled=True)

    def moments_of(member):
        slice_line, line_x, line_y = member
        onehot = (slice_line[:, None] == levels[None, :]).astype(jnp.float32)
        stacked = jnp.stack([jnp.ones_like(line_x), line_x, line_y])
        return jnp.dot(stacked, onehot, precision=highest, preferred_element_type=jnp.float32)

    def lookup(member):
        slice_line, kick_rows = member
        onehot = (slice_line[:, None] == levels[None, :]).astype(jnp.float32)
        return lax.dot_general(
            kick_rows,
            onehot,
            (((1,), (1,)), ((), ())),
            precision=highest,
            preferred_element_type=jnp.float32,
        )

    coords = phase_space
    centroid_rows = []
    for turn_index in range(TURNS):
        slice_row = slice_ids[turn_index]
        moments = lax.map(moments_of, (slice_row, coords[0], coords[2]))
        moments = lax.psum(moments, "mp")
        density = moments[:, 0] / macro_total
        dipole = jnp.stack([moments[:, 1], moments[:, 2]]) / macro_total
        centroid = jnp.sum(dipole, axis=2)
        centroid_rows.append(centroid)
        dip_kick = jnp.einsum("pbj,ij->pbi", dipole, sr_dipole, precision=highest)
        quad_kick = jnp.einsum("bj,ij->bi", density, sr_quad, precision=highest)
        current_all = lax.all_gather(centroid, "bunch", axis=1, tiled=True)
        all_rows = jnp.concatenate([current_all[:, None, :], whole], axis=1)[:, :, ::-1].reshape(
            2, length
        )
        far_kick = jnp.einsum("bk,pk->pb", windows, all_rows, precision=highest)
        whole = jnp.concatenate([current_all[:, None, :], whole[:, :-1]], axis=1)
        kick_table = jnp.stack([dip_kick[0], dip_kick[1], quad_kick], axis=1)
        picked = lax.map(lookup, (slice_row, kick_table))
        coord_x, moment_x, coord_y, moment_y = (coords[0], coords[1], coords[2], coords[3])
        moment_x = moment_x + picked[:, 0] + picked[:, 2] * coord_x + far_kick[0][:, None]
        moment_y = moment_y + picked[:, 1] - picked[:, 2] * coord_y + far_kick[1][:, None]
        action = coord_x * coord_x + moment_x * moment_x + coord_y * coord_y + moment_y * moment_y
        angle_x = phase_advance[0][:, None] + DETUNE * action
        angle_y = phase_advance[1][:, None] + DETUNE * action
        new_x = jnp.cos(angle_x) * coord_x + jnp.sin(angle_x) * moment_x
        new_mx = -jnp.sin(angle_x) * coord_x + jnp.cos(angle_x) * moment_x
        new_y = jnp.cos(angle_y) * coord_y + jnp.sin(angle_y) * moment_y
        new_my = -jnp.sin(angle_y) * coord_y + jnp.cos(angle_y) * moment_y
        coords = jnp.stack([new_x, new_mx, new_y, new_my])
        history = jnp.concatenate([centroid[:, None, :], history[:, :-1]], axis=1)
    return (coords, jnp.stack(centroid_rows, axis=1))


def solution(mesh):
    placed = (
        P(None, "bunch", "mp"),
        P(None, "bunch"),
        P(None, None, "bunch"),
        P(),
        P(),
        P(),
        P(None, "bunch", "mp"),
    )
    return jax.shard_map(
        body,
        mesh=mesh,
        in_specs=placed,
        out_specs=(P(None, "bunch", "mp"), P(None, None, "bunch")),
        check_vma=False,
    )
```

profile of v0, /device:TPU:0, one launch (start us, length us, event | category | flops | bytes accessed | tf_op | source)
XLA Modules:
  0.0 306.1 jit_solution(7244623451006268379)
XLA Ops:
  1.6 9.9 %all_gather.10 = f32[2,64,64]{1,2,0:T(8,128)S(1)} all-gather(f32[2,64,16]{1,2,0:T(8,128)} %param.17), channel_id=1, replica_groups=mesh['bunch'=4,'mp'=8] {'bunch'}, dimensions={2}, use_global_device_ids=true | all-gather | bytes 40960 | tf_op jit(solution)/shard_map/all_gather | solution.py:26
  11.4 28.2 %while.45 = (s32[]{:T(128)}, f32[4224]{0:T(1024)S(1)}, s32[16,1]{0,1:T(1,128)S(1)}, f32[16,4160]{1,0:T(8,128)S(1)}, s32[]{:T(128)}, /*index=5*/s32[]{:T(128)}) while((s32[]{:T(128)}, f32[4224]{0:T(1024)S(1)}, s32[16,1]{0,1:T(1,128)S(1)}, f32[16,4160]{1,0:T(8,128)S(1)}, s32[]{:T(128)}, /*index=5*/s32[]{:T(128)}) %tuple.122), condition=%wide.while_cond, body=%wide.while_body.sunk | while | flops 2 | bytes 99937 | solution.py:22
  39.7 1.8 slice_bitcast_fusion
  41.5 25.6 %while.46 = (s32[]{:T(128)}, f32[16,3,256]{2,0,1:T(8,128)S(1)}, f32[16,4096]{1,0:T(8,128)S(1)}, f32[16,4096]{1,0:T(8,128)S(1)}, s32[16,4096]{1,0:T(8,128)S(1)}, ...) while((s32[]{:T(128)}, f32[16,3,256]{2,0,1:T(8,128)S(1)}, f32[16,4096]{1,0:T(8,128)S(1)}, ...), condition=%wide.region_1.2_spmd.clone, body=%wide.region_0.1_spmd.clone.sunk | while | flops 38821888 | bytes 162961 | solution.py:49
  41.6 1.4 fusion.77
  43.2 1.4 fusion.77
  44.8 1.4 fusion.77
  46.4 1.4 fusion.77
  48.0 1.4 fusion.77
  49.6 1.4 fusion.77
  51.2 1.4 fusion.77
  52.8 1.4 fusion.77
  54.4 1.4 fusion.77
  56.0 1.4 fusion.77
  57.6 1.4 fusion.77
  59.2 1.4 fusion.77
  60.8 1.4 fusion.77
  62.4 1.4 fusion.77
  64.0 1.4 fusion.77
  65.6 1.4 fusion.77
  67.1 27.5 %psum.14 = f32[16,3,256]{2,0,1:T(8,128)S(1)} all-reduce(f32[16,3,256]{2,0,1:T(8,128)S(1)} %get-tuple-element.120), channel_id=1, replica_groups=mesh['bunch'=4,'mp'=8] {'mp'}, use_global_device_ids=true, to_apply=%region_2.3 | all-reduce | flops 12288 | bytes 98304 | tf_op jit(solution)/shard_map/psum | solution.py:50
  95.5 7.7 %all-gather = f32[4,16,2]{1,2,0:T(2,128)S(1)} all-gather(f32[1,16,2]{1,2,0:T(2,128)S(1)} %bitcast.229), channel_id=1, replica_groups=mesh['bunch'=4,'mp'=8] {'bunch'}, dimensions={0}, use_global_device_ids=true | all-gather | bytes 640 | tf_op jit(solution)/shard_map/all_gather | solution.py:57
  104.2 42.7 %while.47 = (s32[]{:T(128)}, f32[16,3,4096]{2,0,1:T(8,128)S(1)}, f32[16,3,256]{2,0,1:T(8,128)S(1)}, s32[16,4096]{1,0:T(8,128)S(1)}, s32[]{:T(128)}, /*index=5*/s32[]{:T(128)}) while((s32[]{:T(128)}, f32[16,3,4096]{2,0,1:T(8,128)S(1)}, f32[16,3,256]{2,0,1:T(8,128)S(1)}, s32[16,4096]{1,0:T(8,128)S(1)}, s32[]{:T(128)}, ...), condition=%wide.region_4.5_spmd.clone, body=%wide.region_3.4_spmd.clone.sunk | while | flops 38797312 | bytes 304217 | solution.py:64
  104.3 2.1 convolution_bitcast_fusion.6
  107.0 2.1 convolution_bitcast_fusion.6
  109.6 2.1 convolution_bitcast_fusion.6
  112.3 2.1 convolution_bitcast_fusion.6
  115.0 2.1 convolution_bitcast_fusion.6
  117.6 2.1 convolution_bitcast_fusion.6
  120.3 2.1 convolution_bitcast_fusion.6
  123.0 2.1 convolution_bitcast_fusion.6
  125.7 2.1 convolution_bitcast_fusion.6
  128.3 2.1 convolution_bitcast_fusion.6
  131.0 2.1 convolution_bitcast_fusion.6
  133.7 2.1 convolution_bitcast_fusion.6
  136.3 2.1 convolution_bitcast_fusion.6
  139.0 2.1 convolution_bitcast_fusion.6
  141.7 2.1 convolution_bitcast_fusion.6
  144.3 2.1 convolution_bitcast_fusion.6
  147.0 3.1 %multiply_add_fusion.5 = (f32[16,4096]{1,0:T(8,128)}, f32[16,4096]{1,0:T(8,128)}) fusion(f32[16]{0:T(128)S(1)} %get-tuple-element.281, f32[16]{0:T(128)S(1)} %get-tuple-element.285, f32[16,3,4096]{2,0,1:T(8,128)S(1)} %get-tuple-element.121, f32[4,16,4096]{2,1,0:T(8,128)S(1)} %copy-done.1, f32[16]{0:T(128)S(1)} %get-tuple-element.286, ...), kind=kLoop, calls=%fused_computation.81 | loop fusion | flops 1572864 | bytes 2359552 | tf_op jit(solution)/shard_map/add | solution.py:73
  150.9 55.3 %while.48 = (s32[]{:T(128)}, f32[16,3,256]{2,0,1:T(8,128)S(1)}, f32[16,4096]{1,0:T(8,128)}, f32[16,4096]{1,0:T(8,128)}, s32[16,4096]{1,0:T(8,128)}, /*index=5*/s32[]{:T(128)}, f32[]{:T(128)}, f32[]{:T(128)}, s32[]{:T(128)}) while((s32[]{:T(128)}, f32[16,3,256]{2,0,1:T(8,128)S(1)}, f32[16,4096]{1,0:T(8,128)}, f32[16,4096]{1,0:T(8,128)}, ...), condition=%wide.region_7.8_spmd.clone, body=%wide.region_6.7_spmd.clone.sunk | while | flops 38821888 | bytes 162961 | solution.py:49
  187.5 1.4 fusion.79
  190.9 1.4 fusion.79
  206.3 26.3 %psum.15 = f32[16,3,256]{2,0,1:T(8,128)S(1)} all-reduce(f32[16,3,256]{2,0,1:T(8,128)S(1)} %get-tuple-element.122), channel_id=1, replica_groups=mesh['bunch'=4,'mp'=8] {'mp'}, use_global_device_ids=true, to_apply=%region_8.9 | all-reduce | flops 12288 | bytes 98304 | tf_op jit(solution)/shard_map/psum | solution.py:50
  234.0 7.5 %all-gather.1 = f32[4,16,2]{1,2,0:T(2,128)S(1)} all-gather(f32[1,16,2]{1,2,0:T(2,128)S(1)} %bitcast.232), channel_id=1, replica_groups=mesh['bunch'=4,'mp'=8] {'bunch'}, dimensions={0}, use_global_device_ids=true | all-gather | bytes 640 | tf_op jit(solution)/shard_map/all_gather | solution.py:57
  242.5 57.1 %while.49 = (s32[]{:T(128)}, f32[16,3,4096]{2,0,1:T(8,128)S(1)}, f32[16,3,256]{2,0,1:T(8,128)S(1)}, s32[16,4096]{1,0:T(8,128)}, s32[]{:T(128)}, /*index=5*/s32[]{:T(128)}) while((s32[]{:T(128)}, f32[16,3,4096]{2,0,1:T(8,128)S(1)}, f32[16,3,256]{2,0,1:T(8,128)S(1)}, s32[16,4096]{1,0:T(8,128)}, s32[]{:T(128)}, ...), condition=%wide.region_10.11_spmd.clone, body=%wide.region_9.10_spmd.clone.sunk | while | flops 38797312 | bytes 304217 | solution.py:64
  243.5 2.1 convolution_bitcast_fusion.7
  247.0 2.1 convolution_bitcast_fusion.7
  250.6 2.1 convolution_bitcast_fusion.7
  254.2 2.1 convolution_bitcast_fusion.7
  257.8 2.1 convolution_bitcast_fusion.7
  261.3 2.1 convolution_bitcast_fusion.7
  264.9 2.1 convolution_bitcast_fusion.7
  268.5 2.1 convolution_bitcast_fusion.7
  272.0 2.1 convolution_bitcast_fusion.7
  275.6 2.1 convolution_bitcast_fusion.7
  279.2 2.1 convolution_bitcast_fusion.7
  282.7 2.1 convolution_bitcast_fusion.7
  286.3 2.1 convolution_bitcast_fusion.7
  289.9 2.1 convolution_bitcast_fusion.7
  293.4 2.1 convolution_bitcast_fusion.7
  297.0 2.1 convolution_bitcast_fusion.7
  299.6 3.3 %multiply_add_fusion.3 = (f32[1,16,4096]{2,1,0:T(8,128)S(1)}, f32[1,16,4096]{2,1,0:T(8,128)S(1)}, f32[1,16,4096]{2,1,0:T(8,128)S(1)}, f32[1,16,4096]{2,1,0:T(8,128)S(1)}, f32[1,16,4096]{2,1,0:T(8,128)S(1)}) fusion(f32[16]{0:T(128)S(1)} %copy-done.4, f32[16]{0:T(128)S(1)} %get-tuple-element.280, f32[16,3,4096]{2,0,1:T(8,128)S(1)} %get-tuple-element.123, ...), kind=kLoop, calls=%fused_computation.77 | loop fusion | flops 2359296 | bytes 3408128 | tf_op jit(solution)/shard_map/add | solution.py:71
  302.9 2.2 multiply_add_fusion.1
  (424 shorter events, 118.6 us)
Async XLA Ops:
  0.6 94.5 %copy-start = (f32[256,256]{1,0:T(8,128)S(1)}, f32[256,256]{1,0:T(8,128)}, u32[]{:S(2)}) copy-start(f32[256,256]{1,0:T(8,128)} %param.19) | copy-start | bytes 786436
  0.6 40.8 %copy-start.1 = (f32[4,16,4096]{2,1,0:T(8,128)S(1)}, f32[4,16,4096]{2,1,0:T(8,128)}, u32[]{:S(2)}) copy-start(f32[4,16,4096]{2,1,0:T(8,128)} %param.15) | copy-start | bytes 3145732
  41.5 53.2 %copy-start.2 = (f32[256,256]{1,0:T(8,128)S(1)}, f32[256,256]{1,0:T(8,128)}, u32[]{:S(2)}) copy-start(f32[256,256]{1,0:T(8,128)} %param.20) | copy-start | bytes 786436
  67.1 37.0 %copy-start.7 = (f32[2,16]{1,0:T(2,128)S(1)}, f32[2,16]{1,0:T(2,128)}, u32[]{:S(2)}) copy-start(f32[2,16]{1,0:T(2,128)} %param.16) | copy-start | bytes 388
  104.1 42.8 %copy-start.3 = (f32[16]{0:T(128)}, f32[16]{0:T(128)S(1)}, u32[]{:S(2)}) copy-start(f32[16]{0:T(128)S(1)} %get-tuple-element.282) | copy-start | bytes 196
  104.2 42.8 %copy-start.5 = (f32[16]{0:T(128)}, f32[16]{0:T(128)S(1)}, u32[]{:S(2)}) copy-start(f32[16]{0:T(128)S(1)} %get-tuple-element.285) | copy-start | bytes 196
  104.2 42.8 %copy-start.6 = (f32[16]{0:T(128)}, f32[16]{0:T(128)S(1)}, u32[]{:S(2)}) copy-start(f32[16]{0:T(128)S(1)} %get-tuple-element.286) | copy-start | bytes 196
  242.5 57.1 %copy-start.4 = (f32[16]{0:T(128)S(1)}, f32[16]{0:T(128)}, u32[]{:S(2)}) copy-start(f32[16]{0:T(128)} %copy-done.3) | copy-start | bytes 196
where the time goes:
time: 307 us; the launch traced here: 306 us
  matrix products  116 us (38%)
  local copies, waits for them, and re-layouts  95.8 us (31%)
  blocking collectives  78.9 us (26%)
  other arithmetic  10.8 us (4%)
  loops' own time  3.22 us (1%)
    dot_general x32, matrix products, lookup(): lax.dot_general(kick_rows, onehot, (((1,), (1,)), ((), ())), precision=hi...  68 us
    psum x2, blocking collectives, body(): moments = lax.psum(moments, 'mp')  53.9 us
    dynamic_slice x96, local copies, waits for them, and re-layouts, body(): moments = lax.map(moments_of, (slice_row, coords[0], coords[2]))  46.8 us
    dot_general x32, matrix products, moments_of(): jnp.dot(stacked, onehot, precision=highest, preferred_element_type=jnp.fl...  46.3 us
    gather x64, local copies, waits for them, and re-layouts  27.8 us
    all_gather x2, blocking collectives, body(): current_all = lax.all_gather(centroid, 'bunch', axis=1, tiled=True)  15.2 us
    dynamic_update_slice x64, local copies, waits for them, and re-layouts, body(): picked = lax.map(lookup, (slice_row, kick_table))  14.9 us
    all_gather x1, blocking collectives, body(): whole = lax.all_gather(centroid_history, 'bunch', axis=2, tiled=True)  9.87 us

commit v1 on v0

--- a/solution.py
+++ b/solution.py
@@ -47,7 +47,7 @@
     for turn_index in range(TURNS):
         slice_row = slice_ids[turn_index]
         moments = lax.map(moments_of, (slice_row, coords[0], coords[2]))
-        moments = lax.psum(moments, "mp")
+        moments = jnp.sum(lax.all_gather(moments, axis_name="mp"), axis=0)
         density = moments[:, 0] / macro_total
         dipole = jnp.stack([moments[:, 1], moments[:, 2]]) / macro_total
         centroid = jnp.sum(dipole, axis=2)

time: 307 us -> 283 us (0.922)
  blocking collectives: 78.9 us -> 54.7 us
    psum x2 -> x0, blocking collectives: 53.9 us -> none  [body(): moments = lax.psum(moments, 'mp')]
    all_gather x0 -> x2, blocking collectives: none -> 29.5 us  [body(): moments = jnp.sum(lax.all_gather(moments, axis_name='mp'), axis=0)]
where the time goes in v1:
time: 283 us; the launch traced here: 282 us
  matrix products  116 us (41%)
  local copies, waits for them, and re-layouts  95.8 us (34%)
  blocking collectives  54.7 us (19%)
  other arithmetic  11 us (4%)
  loops' own time  3.22 us (1%)
    dot_general x32, matrix products, lookup(): lax.dot_general(kick_rows, onehot, (((1,), (1,)), ((), ())), precision=hi...  68 us
    dynamic_slice x96, local copies, waits for them, and re-layouts, body(): moments = lax.map(moments_of, (slice_row, coords[0], coords[2]))  46.8 us
    dot_general x32, matrix products, moments_of(): jnp.dot(stacked, onehot, precision=highest, preferred_element_type=jnp.fl...  46.3 us
    all_gather x2, blocking collectives, body(): moments = jnp.sum(lax.all_gather(moments, axis_name='mp'), axis=0)  29.5 us
    gather x64, local copies, waits for them, and re-layouts  27.8 us
    all_gather x2, blocking collectives, body(): current_all = lax.all_gather(centroid, 'bunch', axis=1, tiled=True)  15.3 us
    dynamic_update_slice x64, local copies, waits for them, and re-layouts, body(): picked = lax.map(lookup, (slice_row, kick_table))  14.9 us
    all_gather x1, blocking collectives, body(): whole = lax.all_gather(centroid_history, 'bunch', axis=2, tiled=True)  9.87 us

profile of v1, /device:TPU:0, one launch (start us, length us, event | category | flops | bytes accessed | tf_op | source)
XLA Modules:
  0.0 282.0 jit_solution(17117864673506331025)
XLA Ops:
  1.6 9.9 %all_gather.24 = f32[2,64,64]{1,2,0:T(8,128)S(1)} all-gather(f32[2,64,16]{1,2,0:T(8,128)} %param.17), channel_id=1, replica_groups=mesh['bunch'=4,'mp'=8] {'bunch'}, dimensions={2}, use_global_device_ids=true | all-gather | bytes 40960 | tf_op jit(solution)/shard_map/all_gather | solution.py:26
  11.4 28.2 %while.45 = (s32[]{:T(128)}, f32[4224]{0:T(1024)S(1)}, s32[16,1]{0,1:T(1,128)S(1)}, f32[16,4160]{1,0:T(8,128)S(1)}, s32[]{:T(128)}, /*index=5*/s32[]{:T(128)}) while((s32[]{:T(128)}, f32[4224]{0:T(1024)S(1)}, s32[16,1]{0,1:T(1,128)S(1)}, f32[16,4160]{1,0:T(8,128)S(1)}, s32[]{:T(128)}, /*index=5*/s32[]{:T(128)}) %tuple.124), condition=%wide.while_cond, body=%wide.while_body.sunk | while | flops 2 | bytes 99937 | solution.py:22
  39.7 1.8 slice_bitcast_fusion
  41.5 25.6 %while.46 = (s32[]{:T(128)}, f32[16,3,256]{2,0,1:T(8,128)S(1)}, f32[16,4096]{1,0:T(8,128)S(1)}, f32[16,4096]{1,0:T(8,128)S(1)}, s32[16,4096]{1,0:T(8,128)S(1)}, ...) while((s32[]{:T(128)}, f32[16,3,256]{2,0,1:T(8,128)S(1)}, f32[16,4096]{1,0:T(8,128)S(1)}, ...), condition=%wide.region_1.2_spmd.clone, body=%wide.region_0.1_spmd.clone.sunk | while | flops 38821888 | bytes 162961 | solution.py:49
  41.6 1.4 fusion.73
  43.2 1.4 fusion.73
  44.8 1.4 fusion.73
  46.4 1.4 fusion.73
  48.0 1.4 fusion.73
  49.6 1.4 fusion.73
  51.2 1.4 fusion.73
  52.8 1.4 fusion.73
  54.4 1.4 fusion.73
  56.0 1.4 fusion.73
  57.6 1.4 fusion.73
  59.2 1.4 fusion.73
  60.8 1.4 fusion.73
  62.4 1.4 fusion.73
  64.0 1.4 fusion.73
  65.6 1.4 fusion.73
  67.1 15.0 %all-gather = f32[128,3,256]{2,0,1:T(8,128)S(1)} all-gather(f32[16,3,256]{2,0,1:T(8,128)S(1)} %get-tuple-element.120), channel_id=2, replica_groups=mesh['bunch'=4,'mp'=8] {'mp'}, dimensions={0}, use_global_device_ids=true | all-gather | bytes 442368 | tf_op jit(solution)/shard_map/all_gather | solution.py:50
  83.0 7.9 %all-gather.2 = f32[4,16,2]{1,2,0:T(2,128)S(1)} all-gather(f32[1,16,2]{1,2,0:T(2,128)S(1)} %bitcast.233), channel_id=1, replica_groups=mesh['bunch'=4,'mp'=8] {'bunch'}, dimensions={0}, use_global_device_ids=true | all-gather | bytes 640 | tf_op jit(solution)/shard_map/all_gather | solution.py:57
  92.0 42.7 %while.47 = (s32[]{:T(128)}, f32[16,3,4096]{2,0,1:T(8,128)S(1)}, f32[16,3,256]{2,0,1:T(8,128)S(1)}, s32[16,4096]{1,0:T(8,128)S(1)}, s32[]{:T(128)}, /*index=5*/s32[]{:T(128)}) while((s32[]{:T(128)}, f32[16,3,4096]{2,0,1:T(8,128)S(1)}, f32[16,3,256]{2,0,1:T(8,128)S(1)}, s32[16,4096]{1,0:T(8,128)S(1)}, s32[]{:T(128)}, ...), condition=%wide.region_4.5_spmd.clone, body=%wide.region_3.4_spmd.clone.sunk | while | flops 38797312 | bytes 304217 | solution.py:64
  92.0 2.1 convolution_bitcast_fusion.6
  94.7 2.1 convolution_bitcast_fusion.6
  97.4 2.1 convolution_bitcast_fusion.6
  100.0 2.1 convolution_bitcast_fusion.6
  102.7 2.1 convolution_bitcast_fusion.6
  105.4 2.1 convolution_bitcast_fusion.6
  108.0 2.1 convolution_bitcast_fusion.6
  110.7 2.1 convolution_bitcast_fusion.6
  113.4 2.1 convolution_bitcast_fusion.6
  116.1 2.1 convolution_bitcast_fusion.6
  118.7 2.1 convolution_bitcast_fusion.6
  121.4 2.1 convolution_bitcast_fusion.6
  124.1 2.1 convolution_bitcast_fusion.6
  126.7 2.1 convolution_bitcast_fusion.6
  129.4 2.1 convolution_bitcast_fusion.6
  132.1 2.1 convolution_bitcast_fusion.6
  134.7 3.1 %multiply_add_fusion.5 = (f32[16,4096]{1,0:T(8,128)}, f32[16,4096]{1,0:T(8,128)}) fusion(f32[16]{0:T(128)S(1)} %get-tuple-element.283, f32[16]{0:T(128)S(1)} %get-tuple-element.287, f32[16,3,4096]{2,0,1:T(8,128)S(1)} %get-tuple-element.121, f32[4,16,4096]{2,1,0:T(8,128)S(1)} %copy-done.1, f32[16]{0:T(128)S(1)} %get-tuple-element.288, ...), kind=kLoop, calls=%fused_computation.81 | loop fusion | flops 1572864 | bytes 2359552 | tf_op jit(solution)/shard_map/add | solution.py:73
  138.7 55.3 %while.48 = (s32[]{:T(128)}, f32[16,3,256]{2,0,1:T(8,128)S(1)}, f32[16,4096]{1,0:T(8,128)}, f32[16,4096]{1,0:T(8,128)}, s32[16,4096]{1,0:T(8,128)}, /*index=5*/s32[]{:T(128)}, f32[]{:T(128)}, f32[]{:T(128)}, s32[]{:T(128)}) while((s32[]{:T(128)}, f32[16,3,256]{2,0,1:T(8,128)S(1)}, f32[16,4096]{1,0:T(8,128)}, f32[16,4096]{1,0:T(8,128)}, ...), condition=%wide.region_7.8_spmd.clone, body=%wide.region_6.7_spmd.clone.sunk | while | flops 38821888 | bytes 162961 | solution.py:49
  157.9 1.4 fusion.75
  161.4 1.4 fusion.75
  194.0 14.5 %all-gather.1 = f32[128,3,256]{2,0,1:T(8,128)S(1)} all-gather(f32[16,3,256]{2,0,1:T(8,128)S(1)} %get-tuple-element.122), channel_id=3, replica_groups=mesh['bunch'=4,'mp'=8] {'mp'}, dimensions={0}, use_global_device_ids=true | all-gather | bytes 442368 | tf_op jit(solution)/shard_map/all_gather | solution.py:50
  210.0 7.4 %all-gather.3 = f32[4,16,2]{1,2,0:T(2,128)S(1)} all-gather(f32[1,16,2]{1,2,0:T(2,128)S(1)} %bitcast.236), channel_id=1, replica_groups=mesh['bunch'=4,'mp'=8] {'bunch'}, dimensions={0}, use_global_device_ids=true | all-gather | bytes 640 | tf_op jit(solution)/shard_map/all_gather | solution.py:57
  218.4 57.1 %while.49 = (s32[]{:T(128)}, f32[16,3,4096]{2,0,1:T(8,128)S(1)}, f32[16,3,256]{2,0,1:T(8,128)S(1)}, s32[16,4096]{1,0:T(8,128)}, s32[]{:T(128)}, /*index=5*/s32[]{:T(128)}) while((s32[]{:T(128)}, f32[16,3,4096]{2,0,1:T(8,128)S(1)}, f32[16,3,256]{2,0,1:T(8,128)S(1)}, s32[16,4096]{1,0:T(8,128)}, s32[]{:T(128)}, ...), condition=%wide.region_10.11_spmd.clone, body=%wide.region_9.10_spmd.clone.sunk | while | flops 38797312 | bytes 304217 | solution.py:64
  219.4 2.1 convolution_bitcast_fusion.7
  223.0 2.1 convolution_bitcast_fusion.7
  226.5 2.1 convolution_bitcast_fusion.7
  230.1 2.1 convolution_bitcast_fusion.7
  233.7 2.1 convolution_bitcast_fusion.7
  237.2 2.1 convolution_bitcast_fusion.7
  240.8 2.1 convolution_bitcast_fusion.7
  244.4 2.1 convolution_bitcast_fusion.7
  247.9 2.1 convolution_bitcast_fusion.7
  251.5 2.1 convolution_bitcast_fusion.7
  255.1 2.1 convolution_bitcast_fusion.7
  258.6 2.1 convolution_bitcast_fusion.7
  262.2 2.1 convolution_bitcast_fusion.7
  265.8 2.1 convolution_bitcast_fusion.7
  269.4 2.1 convolution_bitcast_fusion.7
  272.9 2.1 convolution_bitcast_fusion.7
  275.5 3.3 %multiply_add_fusion.3 = (f32[1,16,4096]{2,1,0:T(8,128)S(1)}, f32[1,16,4096]{2,1,0:T(8,128)S(1)}, f32[1,16,4096]{2,1,0:T(8,128)S(1)}, f32[1,16,4096]{2,1,0:T(8,128)S(1)}, f32[1,16,4096]{2,1,0:T(8,128)S(1)}) fusion(f32[16]{0:T(128)S(1)} %copy-done.4, f32[16]{0:T(128)S(1)} %get-tuple-element.282, f32[16,3,4096]{2,0,1:T(8,128)S(1)} %get-tuple-element.123, ...), kind=kLoop, calls=%fused_computation.77 | loop fusion | flops 2359296 | bytes 3408128 | tf_op jit(solution)/shard_map/add | solution.py:71
  278.8 2.2 multiply_add_fusion.1
  (428 shorter events, 118.7 us)
Async XLA Ops:
  0.6 82.0 %copy-start = (f32[256,256]{1,0:T(8,128)S(1)}, f32[256,256]{1,0:T(8,128)}, u32[]{:S(2)}) copy-start(f32[256,256]{1,0:T(8,128)} %param.19) | copy-start | bytes 786436
  0.6 40.8 %copy-start.1 = (f32[4,16,4096]{2,1,0:T(8,128)S(1)}, f32[4,16,4096]{2,1,0:T(8,128)}, u32[]{:S(2)}) copy-start(f32[4,16,4096]{2,1,0:T(8,128)} %param.15) | copy-start | bytes 3145732
  67.1 15.1 %copy-start.2 = (f32[256,256]{1,0:T(8,128)S(1)}, f32[256,256]{1,0:T(8,128)}, u32[]{:S(2)}) copy-start(f32[256,256]{1,0:T(8,128)} %param.20) | copy-start | bytes 786436
  82.2 9.7 %copy-start.7 = (f32[2,16]{1,0:T(2,128)S(1)}, f32[2,16]{1,0:T(2,128)}, u32[]{:S(2)}) copy-start(f32[2,16]{1,0:T(2,128)} %param.16) | copy-start | bytes 388
  91.9 42.8 %copy-start.3 = (f32[16]{0:T(128)}, f32[16]{0:T(128)S(1)}, u32[]{:S(2)}) copy-start(f32[16]{0:T(128)S(1)} %get-tuple-element.284) | copy-start | bytes 196
  91.9 42.8 %copy-start.5 = (f32[16]{0:T(128)}, f32[16]{0:T(128)S(1)}, u32[]{:S(2)}) copy-start(f32[16]{0:T(128)S(1)} %get-tuple-element.287) | copy-start | bytes 196
  91.9 42.8 %copy-start.6 = (f32[16]{0:T(128)}, f32[16]{0:T(128)S(1)}, u32[]{:S(2)}) copy-start(f32[16]{0:T(128)S(1)} %get-tuple-element.288) | copy-start | bytes 196
  218.4 57.1 %copy-start.4 = (f32[16]{0:T(128)S(1)}, f32[16]{0:T(128)}, u32[]{:S(2)}) copy-start(f32[16]{0:T(128)} %copy-done.3) | copy-start | bytes 196
